TPU v7x, 32 devices: a whole 2x2x4 slice. The times are simulated.
32 devices in a mesh: groups: 2 (over x), mset: 16 (over z, y, core).
Axes of the slice: x: 2, y: 2, z: 4, core: 2. Of those that a mesh axis runs over, the one named last changes fastest.
Arguments:
- m_list: int32 [16], replicated, may hold values from 1536 to 3071, as said below
- coeff: bfloat16 [32, 32, 1536], P(('groups', 'mset')), parts along dimension 0, may hold values from -6 to 6
- blocks: bfloat16 [32, 1536, 1536], P(('groups', 'mset')), parts along dimension 0, may hold values from -0.15625 to 0.15625
- legendre: bfloat16 [512, 16, 1536], P(('groups', 'mset')), parts along dimension 0, may hold values from -0.15625 to 0.15625
Outputs:
- sky_map: bfloat16 [512, 16, 8192], P(('groups', 'mset')), parts along dimension 0
There are 2 independent parts, one for each index of `groups`. A program takes and returns all parts, laid end to end along the dimension named above; an argument that names none is the same for every part. Nothing has to cross between parts.
Inputs may be any that keep to these rules, and one draw needn't show every extreme that they name: `m_list`: 16 distinct values; the value 3072 - 1536, a block of full order 1536, is always among them.
All inputs are finite; a program needn't handle non-finite values.
Results may differ from a plain program's by a relative error of at most 0.0062.
Values may be sent and summed in bfloat16 or wider, within the bound.
A program may use at most 64 MiB of HBM per device.

v0:
```python
import math

import jax
import jax.numpy as jnp
from jax import lax
from jax.sharding import PartitionSpec as P

LL = 3072
REAL = 16
NPHI = 8192


def fourier_table(m_values, pixels):
    pixel_index = jnp.arange(pixels, dtype=jnp.int32)
    phases = m_values[:, None] * pixel_index[None, :] % pixels
    angles = phases.astype(jnp.float32) * (2.0 * math.pi / pixels)
    cos_part = jnp.cos(angles).astype(jnp.bfloat16)
    sin_part = jnp.sin(angles).astype(jnp.bfloat16)
    return jnp.concatenate([cos_part, -sin_part], axis=0)


def body(m_list, coeff, blocks, legendre):
    per_device = coeff.shape[0]
    order_max = coeff.shape[2]
    first_slot = lax.axis_index("mset") * per_device
    own_m = lax.dynamic_slice_in_dim(m_list, first_slot, per_device)
    orders = LL - own_m
    valid_mask = jnp.arange(order_max, dtype=jnp.int32)[None, :] < orders[:, None]
    masked = jnp.where(valid_mask[:, None, :], coeff, jnp.zeros_like(coeff))
    products = jnp.einsum("mcj,mjk->mck", masked, blocks, preferred_element_type=jnp.float32)
    filtered = jnp.where(valid_mask[:, None, :], products, jnp.zeros_like(products)).astype(
        jnp.bfloat16
    )
    tables = lax.all_to_all(legendre, "mset", split_axis=1, concat_axis=0, tiled=True)
    local_part = jnp.einsum(
        "rmj,mcj->rmc", tables, filtered, preferred_element_type=jnp.float32
    ).astype(jnp.bfloat16)
    harmonics = lax.all_to_all(local_part, "mset", split_axis=0, concat_axis=1, tiled=True)
    cycle_count = harmonics.shape[0]
    subset_size = m_list.shape[0]
    real_part = harmonics[:, :, :REAL]
    imag_part = harmonics[:, :, REAL:]
    stacked = jnp.concatenate([real_part, imag_part], axis=1)
    flattened = jnp.transpose(stacked, (0, 2, 1)).reshape(cycle_count * REAL, 2 * subset_size)
    trig_table = fourier_table(m_list, NPHI)
    summed_map = jnp.dot(flattened, trig_table, preferred_element_type=jnp.float32)
    scaled = summed_map * (1.0 / math.sqrt(subset_size))
    return scaled.astype(jnp.bfloat16).reshape(cycle_count, REAL, NPHI)


def solution(mesh):
    in_specs = (
        P(),
        P(("groups", "mset"), None, None),
        P(("groups", "mset"), None, None),
        P(("groups", "mset"), None, None),
    )
    out_specs = P(("groups", "mset"), None, None)
    return jax.shard_map(body, mesh=mesh, in_specs=in_specs, out_specs=out_specs, check_vma=False)
```

profile of v0, /device:TPU:0, one launch (start us, length us, event | category | flops | bytes accessed | tf_op | source)
XLA Modules:
  0.0 49.7 jit_solution(17770142422807832663)
XLA Ops:
  0.0 0.0 copy-start
  0.0 2.5 %copy.8 = bf16[16,16,1536]{2,0,1:T(8,128)(2,1)} copy(bf16[16,16,1536]{2,1,0:T(8,128)(2,1)} %param.7) | data formatting | bytes 1572864 | tf_op args[3]
  2.5 7.4 %all-to-all-start = ((bf16[16,16,1536]{2,0,1:T(8,128)(2,1)}), bf16[16,16,1536]{2,0,1:T(8,128)(2,1)S(1)}, u32[]{:S(2)}, u32[]{:S(2)}) async-start(bf16[16,16,1536]{2,0,1:T(8,128)(2,1)} %copy.8), calls=%async_computation | async-start | bytes 1572864 | tf_op jit(solution)/shard_map/all_to_all | solution.py:34
  9.9 1.3 %dynamic_slice.3 = s32[1]{0:T(128)} dynamic-slice(s32[16]{0:T(128)} %param.4, s32[]{:T(128)S(6)} %select_n.19), dynamic_slice_sizes={1} | dynamic-slice | bytes 12 | tf_op jit(solution)/shard_map/dynamic_slice | solution.py:26
  11.8 2.8 %fusion.27 = bf16[16,8192]{1,0:T(8,128)(2,1)S(1)} fusion(s32[16]{0:T(128)} %param.4), kind=kLoop, calls=%fused_computation.23 | loop fusion | flops 2359296 | bytes 262208 | tf_op jit(solution)/shard_map/neg | solution.py:19
  14.6 14.0 %all-to-all-done = bf16[16,16,1536]{2,0,1:T(8,128)(2,1)S(1)} async-done(((bf16[16,16,1536]{2,0,1:T(8,128)(2,1)}), bf16[16,16,1536]{2,0,1:T(8,128)(2,1)S(1)}, u32[]{:S(2)}, u32[]{:S(2)}) %all-to-all-start) | async-done | bytes 786464 | tf_op jit(solution)/shard_map/all_to_all | solution.py:34
  28.6 3.5 %fusion.15 = bf16[256,1,32]{0,2,1:T(8,128)(2,1)S(1)} fusion(bf16[256,1536]{1,0:T(8,128)(2,1)S(1)} %bitcast.38, bf16[1,1536,1536]{2,1,0:T(8,128)(2,1)} %param.6, bf16[1,32,1536]{2,1,0:T(8,128)(2,1)} %param.5, pred[1536]{0:T(1024)(128)(4,1)S(1)} %iota_compare_fusion), kind=kOutput, calls=%fused_computation.8 | convolution fusion | flops 176316416 | bytes 5621248 | tf_op jit(solution)/shard_map/rmj,mcj->rmc/dot_general | solution.py:35
  32.1 0.5 %broadcast.23 = bf16[]{:T(256)} broadcast(bf16[]{:T(256)} %constant.70), dimensions={} | broadcast | bytes 4 | tf_op jit(solution)/shard_map/convert_element_type | solution.py:37
  32.6 0.7 %reduce = bf16[256,32]{0,1:T(8,128)(2,1)S(1)} reduce(bf16[256,1,32]{0,2,1:T(8,128)(2,1)S(1)} %fusion.15, bf16[]{:T(256)} %broadcast.23), dimensions={1}, to_apply=%copy.9.reduce_sub_computation | reduce | bytes 32770 | tf_op jit(solution)/shard_map/convert_element_type | solution.py:37
  33.3 0.1 copy.12
  33.4 0.7 %reshape.40 = bf16[16,2,256]{2,1,0:T(2,128)(2,1)} reshape(bf16[256,32]{1,0:T(8,128)(2,1)S(1)} %copy.12) | data formatting | bytes 32768
  34.1 5.4 %all-to-all-start.1 = ((bf16[16,2,256]{2,1,0:T(2,128)(2,1)}), bf16[16,2,256]{2,1,0:T(2,128)(2,1)S(1)}, u32[]{:S(2)}, u32[]{:S(2)}) async-start(bf16[16,2,256]{2,1,0:T(2,128)(2,1)} %reshape.40), calls=%async_computation.1 | async-start | bytes 32768 | tf_op jit(solution)/shard_map/all_to_all | solution.py:38
  39.5 0.0 copy-done
  39.5 2.1 %cosine_convert_fusion = bf16[16,8192]{1,0:T(8,128)(2,1)S(1)} fusion(s32[16]{0:T(128)S(1)} %copy-done), kind=kLoop, calls=%fused_computation.19 | loop fusion | flops 1966080 | bytes 262208 | tf_op jit(solution)/shard_map/convert_element_type | solution.py:17
  41.6 4.4 %all-to-all-done.1 = bf16[16,2,256]{2,1,0:T(2,128)(2,1)S(1)} async-done(((bf16[16,2,256]{2,1,0:T(2,128)(2,1)}), bf16[16,2,256]{2,1,0:T(2,128)(2,1)S(1)}, u32[]{:S(2)}, u32[]{:S(2)}) %all-to-all-start.1) | async-done | bytes 16416 | tf_op jit(solution)/shard_map/all_to_all | solution.py:38
  46.0 0.1 reshape.41
  46.1 0.1 fusion.42
  46.3 0.2 copy.10
  46.4 3.2 %fusion = bf16[256,8192]{1,0:T(8,128)(2,1)} fusion(bf16[256,32]{1,0:T(8,128)(2,1)S(1)} %bitcast.40, bf16[16,8192]{1,0:T(8,128)(2,1)S(1)} %fusion.27, bf16[16,8192]{1,0:T(8,128)(2,1)S(1)} %cosine_convert_fusion), kind=kOutput, calls=%fused_computation.1 | convolution fusion | flops 139460608 | bytes 4734976 | tf_op jit(solution)/shard_map/dot_general | solution.py:46
  (3 shorter events, 0.0 us)
Async XLA Ops:
  0.0 39.5 %copy-start = (s32[16]{0:T(128)S(1)}, s32[16]{0:T(128)}, u32[]{:S(2)}) copy-start(s32[16]{0:T(128)} %param.4) | copy-start | bytes 196
  2.5 26.1 %all-to-all-start = ((bf16[16,16,1536]{2,0,1:T(8,128)(2,1)}), bf16[16,16,1536]{2,0,1:T(8,128)(2,1)S(1)}, u32[]{:S(2)}, u32[]{:S(2)}) async-start(bf16[16,16,1536]{2,0,1:T(8,128)(2,1)} %copy.8), calls=%async_computation | async-start | bytes 1572864 | tf_op jit(solution)/shard_map/all_to_all | solution.py:34
  34.1 11.9 %all-to-all-start.1 = ((bf16[16,2,256]{2,1,0:T(2,128)(2,1)}), bf16[16,2,256]{2,1,0:T(2,128)(2,1)S(1)}, u32[]{:S(2)}, u32[]{:S(2)}) async-start(bf16[16,2,256]{2,1,0:T(2,128)(2,1)} %reshape.40), calls=%async_computation.1 | async-start | bytes 32768 | tf_op jit(solution)/shard_map/all_to_all | solution.py:38
where the time goes:
time: 50 us; the launch traced here: 49.7 us
  waiting for transfers between devices  18.3 us (37%)
  starting transfers between devices  12.8 us (26%)
  matrix products  6.75 us (14%)
  other arithmetic  5.6 us (11%)
  local copies, waits for them, and re-layouts  5.49 us (11%)
  between operations  0.71 us (1%)
    all_to_all x1, waiting for transfers between devices, body(): lax.all_to_all(legendre, 'mset', split_axis=1, concat_axis=0, tiled=True)  14 us
    all_to_all x1, starting transfers between devices, body(): lax.all_to_all(legendre, 'mset', split_axis=1, concat_axis=0, tiled=True)  7.41 us
    all_to_all x1, starting transfers between devices, body(): lax.all_to_all(local_part, 'mset', split_axis=0, concat_axis=1, tiled=True)  5.38 us
    all_to_all x1, waiting for transfers between devices, body(): lax.all_to_all(local_part, 'mset', split_axis=0, concat_axis=1, tiled=True)  4.38 us
    dot_general x1, matrix products, body(): jnp.einsum('rmj,mcj->rmc', tables, filtered, preferred_element_type=jnp.f...  3.51 us
    unnamed x7, local copies, waits for them, and re-layouts  3.42 us
    dot_general x1, matrix products, body(): jnp.dot(flattened, trig_table, preferred_element_type=jnp.float32)  3.24 us
    neg x1, other arithmetic, fourier_table(): return jnp.concatenate([cos_part, -sin_part], axis=0)  2.81 us
  transfers between devices with their start and end apart: 2, of which 2 were waited for; matrix products, arithmetic and copies ran while one was open for 12% of the time, Pallas kernels for 0%

commit v1 on v0

v1 whole, which is shorter than its diff:
```python
import functools
import math

import jax
import jax.numpy as jnp
from jax import lax
from jax.experimental import pallas as pl
from jax.experimental.pallas import tpu as pltpu
from jax.sharding import PartitionSpec as P

LL = 3072
REAL = 16
NPHI = 8192
LANES = 128
MESH = pl.DeviceIdType.MESH
F32 = jnp.float32
BF16 = jnp.bfloat16


def iota(shape, dim):
    return lax.broadcasted_iota(jnp.int32, shape, dim)


def split_index(x, size):
    if size & (size - 1) == 0:
        shift = size.bit_length() - 1
        return lax.shift_right_logical(x, jnp.int32(shift)), lax.bitwise_and(x, jnp.int32(size - 1))
    quotient = x // size
    return quotient, x - quotient * size


def harmonics_kernel(
    n, chunks, m_ref, coeff_ref, blocks_ref, leg_ref, out_ref, table_ref,
    coeff_v, blocks_v, leg_v, gathered, expand, acc,
    load_sem, recv_sem, up_sem, down_sem, side_sem, sib_sem,
):
    subset = m_ref.shape[0]
    cols, order_max = coeff_ref.shape[1], coeff_ref.shape[2]
    width = order_max // chunks
    group = 4
    depth = n // group
    rows_in = leg_ref.shape[0]
    rows_out = out_ref.shape[0]
    cycles = rows_in // subset
    me = lax.axis_index("mset")
    core = lax.rem(me, 2)
    side = lax.rem(lax.div(me, 2), 2)
    z = lax.div(me, group)
    sibling = me + 1 - 2 * core
    partner = me + 2 - 4 * side

    def load_block(q):
        return pltpu.make_async_copy(
            blocks_ref.at[0, :, pl.ds(q * width, width)], blocks_v.at[q], load_sem.at[q]
        )

    coeff_load = pltpu.make_async_copy(coeff_ref.at[0], coeff_v, load_sem.at[chunks])
    leg_load = pltpu.make_async_copy(leg_ref, leg_v, load_sem.at[chunks + 1])
    coeff_load.start()
    for q in range(chunks):
        load_block(q).start()
    leg_load.start()

    barrier = pltpu.get_barrier_semaphore()

    def greet(target):
        pl.semaphore_signal(barrier, inc=1, device_id={"mset": target}, device_id_type=MESH)

    greet(sibling)
    greet(partner)

    @pl.when(z > 0)
    def _():
        greet(me - group)

    @pl.when(z < depth - 1)
    def _():
        greet(me + group)

    def piece(src, q):
        return gathered.at[src, :, pl.ds(q * width, width)]

    def copy(src, q, target, send_sem):
        return pltpu.make_async_remote_copy(
            src_ref=piece(src, q),
            dst_ref=piece(src, q),
            send_sem=send_sem,
            recv_sem=recv_sem.at[q, src],
            device_id={"mset": target},
            device_id_type=MESH,
        )

    def to_up(src, q):
        return copy(src, q, me + group, up_sem.at[q, lax.div(src, group)])

    def to_down(src, q):
        return copy(src, q, me - group, down_sem.at[q, lax.div(src, group)])

    def to_side(src, q):
        return copy(src, q, partner, side_sem.at[q, lax.div(src, group)])

    def to_sib(src, q):
        return copy(src, q, sibling, sib_sem.at[q, lax.div(src, 2)])

    def arrive(src, q):
        copy(src, q, sibling, sib_sem.at[q, lax.div(src, 2)]).wait_recv()

    order = LL - m_ref[me]
    coeff_load.wait()
    masked = jnp.where(iota((cols, order_max), 1) < order, coeff_v[...].astype(F32), 0.0).astype(BF16)
    for q in range(chunks):
        load_block(q).wait()
        product = jnp.dot(masked, blocks_v[q], preferred_element_type=F32)
        valid = iota((cols, width), 1) + q * width < order
        gathered[me, :, pl.ds(q * width, width)] = jnp.where(valid, product, 0.0).astype(BF16)
        if q == 0:
            peers = 2 + jnp.where(z > 0, 1, 0) + jnp.where(z < depth - 1, 1, 0)
            pl.semaphore_wait(barrier, peers)

        to_side(me, q).start()

        @pl.when(z < depth - 1)
        def _():
            to_up(me, q).start()

        @pl.when(z > 0)
        def _():
            to_down(me, q).start()

        to_sib(me, q).start()

    m_col = jnp.zeros((subset, LANES), jnp.int32)
    slot = iota((subset, LANES), 0)
    for i in range(subset):
        m_col = jnp.where(slot == i, m_ref[i], m_col)
    lane = iota((subset, LANES), 1)
    fine = split_index(m_col * lane, NPHI)[1].astype(F32) * (2.0 * math.pi / NPHI)
    coarse = split_index(m_col * (lane * LANES), NPHI)[1].astype(F32) * (2.0 * math.pi / NPHI)
    fine_cos, fine_sin = jnp.cos(fine), jnp.sin(fine)
    coarse_cos, coarse_sin = jnp.cos(coarse), jnp.sin(coarse)
    for a in range(NPHI // LANES):
        c = coarse_cos[:, a : a + 1]
        s = coarse_sin[:, a : a + 1]
        table_ref[0:subset, a * LANES : (a + 1) * LANES] = (c * fine_cos - s * fine_sin).astype(BF16)
        table_ref[subset : 2 * subset, a * LANES : (a + 1) * LANES] = (
            -(s * fine_cos + c * fine_sin)
        ).astype(BF16)

    out_cycle = split_index(iota((rows_out, rows_in), 0), REAL)[0]
    in_cycle = split_index(iota((rows_out, rows_in), 1), subset)[0]
    expand[...] = jnp.where(out_cycle == in_cycle, 1.0, 0.0).astype(BF16)
    acc[...] = jnp.zeros_like(acc)
    leg_load.wait()

    span = group * cols

    def absorb(zz):
        values = gathered[pl.ds(zz * group, group)].reshape(span, order_max)
        cross = lax.dot_general(
            leg_v[...], values, (((1,), (1,)), ((), ())), preferred_element_type=F32
        )
        row_m = split_index(iota((rows_in, span), 0), subset)[1]
        col_m = split_index(iota((rows_in, span), 1), cols)[0] + zz * group
        own = jnp.where(row_m == col_m, cross, 0.0).astype(BF16)
        spread = jnp.dot(expand[...], own, preferred_element_type=F32)
        row_s = split_index(iota((rows_out, span), 0), REAL)[1]
        col_s = split_index(iota((rows_out, span), 1), REAL)[1]
        picked = jnp.where(row_s == col_s, spread, 0.0).astype(BF16)
        src = iota((span, 2 * subset), 0)
        src_m, src_c = split_index(src, cols)
        dst_part, dst_m = split_index(iota((span, 2 * subset), 1), subset)
        hit = (src_m + zz * group == dst_m) & (split_index(src_c, REAL)[0] == dst_part)
        select = jnp.where(hit, 1.0, 0.0).astype(BF16)
        acc[...] += jnp.dot(picked, select, preferred_element_type=F32)

    def row(zz):
        return zz * group + side * 2 + core, zz * group + (1 - side) * 2 + core

    def finish(zz):
        for s in range(2):
            for q in range(chunks):
                arrive(zz * group + s * 2 + 1 - core, q)
        absorb(zz)

    def relay_line(zz, forward):
        mine, _ = row(zz)
        for q in range(chunks):
            arrive(mine, q)
            forward(mine, q)
            to_side(mine, q).start()
            to_sib(mine, q).start()

    def relay_side(zz):
        _, other = row(zz)
        for q in range(chunks):
            arrive(other, q)
            to_sib(other, q).start()

    def below(d):
        def forward(src, q):
            @pl.when(z < depth - 1)
            def _():
                to_up(src, q).start()

        relay_line(z - d, forward)

    def above(d):
        def forward(src, q):
            @pl.when(z > 0)
            def _():
                to_down(src, q).start()

        relay_line(z + d, forward)

    if depth > 1:
        pl.when(z >= 1)(lambda: below(1))
        pl.when(z <= depth - 2)(lambda: above(1))
    relay_side(z)
    finish(z)
    for d in range(1, depth):
        if d + 1 < depth:
            pl.when(z >= d + 1)(functools.partial(below, d + 1))
            pl.when(z <= depth - 2 - d)(functools.partial(above, d + 1))
        pl.when(z >= d)(functools.partial(lambda d: relay_side(z - d), d))
        pl.when(z <= depth - 1 - d)(functools.partial(lambda d: relay_side(z + d), d))
        pl.when(z >= d)(functools.partial(lambda d: finish(z - d), d))
        pl.when(z <= depth - 1 - d)(functools.partial(lambda d: finish(z + d), d))

    out_ref[...] = acc[...].astype(BF16)

    for zz in range(depth):
        mine, other = row(zz)
        for q in range(chunks):
            to_side(mine, q).wait_send()
            to_sib(mine, q).wait_send()
            to_sib(other, q).wait_send()

            @pl.when((z < depth - 1) & (zz <= z))
            def _():
                to_up(mine, q).wait_send()

            @pl.when((z > 0) & (zz >= z))
            def _():
                to_down(mine, q).wait_send()


def synthesis_kernel(tiles, scale, h_ref, table_ref, out_ref, buf, sem):
    tile = out_ref.shape[1] // tiles
    copies = []
    for t in range(tiles):
        cut = slice(t * tile, (t + 1) * tile)
        total = jnp.dot(h_ref[...], table_ref[:, cut], preferred_element_type=F32)
        buf[:, cut] = (total * scale).astype(BF16)
        copies.append(pltpu.make_async_copy(buf.at[:, cut], out_ref.at[:, cut], sem.at[t]))
        copies[-1].start()
    for c in copies:
        c.wait()


def body(n, m_list, coeff, blocks, legendre):
    per_device, cols, order_max = coeff.shape
    assert per_device == 1 and n % 4 == 0
    cycles, subset, _ = legendre.shape
    chunks = 3
    depth = n // 4
    rows_in, rows_out = cycles * subset, cycles * REAL
    vmem = pl.BlockSpec(memory_space=pltpu.VMEM)
    hbm = pl.BlockSpec(memory_space=pl.ANY)
    dma = pltpu.SemaphoreType.DMA
    harmonics, table = pl.pallas_call(
        functools.partial(harmonics_kernel, n, chunks),
        out_shape=(
            jax.ShapeDtypeStruct((rows_out, 2 * subset), BF16),
            jax.ShapeDtypeStruct((2 * subset, NPHI), BF16),
        ),
        in_specs=[pl.BlockSpec(memory_space=pltpu.SMEM), hbm, hbm, hbm],
        out_specs=(vmem, vmem),
        scratch_shapes=[
            pltpu.VMEM((cols, order_max), BF16),
            pltpu.VMEM((chunks, order_max, order_max // chunks), BF16),
            pltpu.VMEM((rows_in, order_max), BF16),
            pltpu.VMEM((n, cols, order_max), BF16),
            pltpu.VMEM((rows_out, rows_in), BF16),
            pltpu.VMEM((rows_out, 2 * subset), F32),
            dma((chunks + 2,)),
            dma((chunks, n)),
            dma((chunks, depth)),
            dma((chunks, depth)),
            dma((chunks, depth)),
            dma((chunks, 2 * depth)),
        ],
        compiler_params=pltpu.CompilerParams(collective_id=0, has_side_effects=True),
        name="harmonics",
    )(m_list, coeff, blocks, legendre.reshape(rows_in, order_max))
    tiles = 8
    sky = pl.pallas_call(
        functools.partial(synthesis_kernel, tiles, 1.0 / math.sqrt(subset)),
        out_shape=jax.ShapeDtypeStruct((rows_out, NPHI), BF16),
        in_specs=[vmem, vmem],
        out_specs=hbm,
        scratch_shapes=[pltpu.VMEM((rows_out, NPHI), BF16), dma((tiles,))],
        name="synthesis",
    )(harmonics, table)
    return sky.reshape(cycles, REAL, NPHI)


def solution(mesh):
    spec = P(("groups", "mset"), None, None)
    return jax.shard_map(
        functools.partial(body, mesh.shape["mset"]),
        mesh=mesh,
        in_specs=(P(), spec, spec, spec),
        out_specs=spec,
        check_vma=False,
    )
```

time: 50 us -> 25.9 us (0.52)
  the two profiles are of different devices: /device:TPU:0 before, /device:TPU:1 now
where the time goes in v1:
time: 25.9 us; the launch traced here: 25.8 us
  Pallas kernels  25.8 us (100%)
    pallas_call x1, Pallas kernels, body(): pl.pallas_call(functools.partial(harmonics_kernel, n, chunks), out_shape=...  22.4 us
    pallas_call x1, Pallas kernels, body(): pl.pallas_call(functools.partial(synthesis_kernel, tiles, 1.0 / math.sqrt...  3.42 us

profile of v1, /device:TPU:1, one launch (start us, length us, event | category | flops | bytes accessed | tf_op | source)
XLA Modules:
  0.0 25.8 jit_solution(14605031953565451657)
XLA Ops:
  0.0 22.4 %harmonics.1 = (bf16[256,32]{1,0:T(8,128)(2,1)}, bf16[32,8192]{1,0:T(8,128)(2,1)}) custom-call(s32[16]{0:T(128)} %m_ref.1, bf16[1,32,1536]{2,1,0:T(8,128)(2,1)} %coeff_ref.1, bf16[1,1536,1536]{2,1,0:T(8,128)(2,1)} %blocks_ref.1, bf16[256,1536]{1,0:T(8,128)(2,1)} %bitcast.2), custom_call_target="tpu_custom_call" | custom-call | tf_op jit(solution)/shard_map/harmonics/pallas_call | solution.py:270
  22.4 3.4 %synthesis.1 = bf16[256,8192]{1,0:T(8,128)(2,1)} custom-call(bf16[256,32]{1,0:T(8,128)(2,1)} %get-tuple-element.7.h_ref, bf16[32,8192]{1,0:T(8,128)(2,1)} %get-tuple-element.8.table_ref), custom_call_target="tpu_custom_call" | custom-call | tf_op jit(solution)/shard_map/synthesis/pallas_call | solution.py:296

commit v2 on v1

v2 whole, which is shorter than its diff:
```python
import functools
import math

import jax
import jax.numpy as jnp
from jax import lax
from jax.experimental import pallas as pl
from jax.experimental.pallas import tpu as pltpu
from jax.sharding import PartitionSpec as P

LL = 3072
REAL = 16
NPHI = 8192
LANES = 128
MESH = pl.DeviceIdType.MESH
F32 = jnp.float32
BF16 = jnp.bfloat16


def iota(shape, dim):
    return lax.broadcasted_iota(jnp.int32, shape, dim)


def split_index(x, size):
    if size & (size - 1) == 0:
        shift = size.bit_length() - 1
        return lax.shift_right_logical(x, jnp.int32(shift)), lax.bitwise_and(x, jnp.int32(size - 1))
    quotient = x // size
    return quotient, x - quotient * size


def harmonics_kernel(
    n, chunks, m_ref, coeff_ref, blocks_ref, leg_ref, out_ref,
    coeff_v, blocks_v, leg_v, leg_away, leg_here, gathered, harm_away, harm,
    load_sem, recv_sem, up_sem, down_sem, sib_sem, leg_send, leg_recv, harm_sem,
):
    subset = m_ref.shape[0]
    cols, order_max = coeff_ref.shape[1], coeff_ref.shape[2]
    width = order_max // chunks
    group = 4
    depth = n // group
    line = 2 * depth
    rows_in = leg_ref.shape[0]
    rows_out = out_ref.shape[0]
    cycles = rows_in // subset
    rows_half = cycles * line
    span = line * cols
    me = lax.axis_index("mset")
    core = lax.rem(me, 2)
    side = lax.rem(lax.div(me, 2), 2)
    z = lax.div(me, group)
    sibling = me + 1 - 2 * core
    partner = me + 2 - 4 * side

    def load_block(q):
        return pltpu.make_async_copy(
            blocks_ref.at[0, :, pl.ds(q * width, width)], blocks_v.at[q], load_sem.at[q]
        )

    coeff_load = pltpu.make_async_copy(coeff_ref.at[0], coeff_v, load_sem.at[chunks])
    leg_load = pltpu.make_async_copy(leg_ref, leg_v, load_sem.at[chunks + 1])
    coeff_load.start()
    for q in range(chunks):
        load_block(q).start()
    leg_load.start()

    barrier = pltpu.get_barrier_semaphore()

    def greet(target):
        pl.semaphore_signal(barrier, inc=1, device_id={"mset": target}, device_id_type=MESH)

    greet(sibling)
    greet(partner)

    @pl.when(z > 0)
    def _():
        greet(me - group)

    @pl.when(z < depth - 1)
    def _():
        greet(me + group)

    def piece(pos, q):
        return gathered.at[q, pos]

    def copy(pos, q, target, send_sem):
        return pltpu.make_async_remote_copy(
            src_ref=piece(pos, q),
            dst_ref=piece(pos, q),
            send_sem=send_sem,
            recv_sem=recv_sem.at[q, pos],
            device_id={"mset": target},
            device_id_type=MESH,
        )

    def to_up(zz, q):
        return copy(2 * zz + core, q, me + group, up_sem.at[q, zz])

    def to_down(zz, q):
        return copy(2 * zz + core, q, me - group, down_sem.at[q, zz])

    def to_sib(zz, q):
        return copy(2 * zz + core, q, sibling, sib_sem.at[q, zz])

    def arrive(pos, q):
        copy(pos, q, sibling, sib_sem.at[q, 0]).wait_recv()

    def leg_copy(q):
        return pltpu.make_async_remote_copy(
            src_ref=leg_away.at[:, pl.ds(q * width, width)],
            dst_ref=leg_here.at[1, :, pl.ds(q * width, width)],
            send_sem=leg_send.at[q],
            recv_sem=leg_recv.at[q],
            device_id={"mset": partner},
            device_id_type=MESH,
        )

    def side_rows(which):
        row_cycle, row_pos = split_index(iota((rows_half, rows_in), 0), line)
        row_zz, row_core = split_index(row_pos, 2)
        wanted = row_cycle * subset + row_zz * group + which * 2 + row_core
        return jnp.where(iota((rows_half, rows_in), 1) == wanted, 1.0, 0.0).astype(BF16)

    order = LL - m_ref[me]
    coeff_load.wait()
    masked = jnp.where(iota((cols, order_max), 1) < order, coeff_v[...].astype(F32), 0.0).astype(BF16)
    for q in range(chunks):
        load_block(q).wait()
        product = jnp.dot(masked, blocks_v[q], preferred_element_type=F32)
        valid = iota((cols, width), 1) + q * width < order
        gathered[q, 2 * z + core] = jnp.where(valid, product, 0.0).astype(BF16)

        if q == 0:
            peers = 2 + jnp.where(z > 0, 1, 0) + jnp.where(z < depth - 1, 1, 0)
            pl.semaphore_wait(barrier, peers)

        @pl.when(z < depth - 1)
        def _():
            to_up(z, q).start()

        @pl.when(z > 0)
        def _():
            to_down(z, q).start()

        to_sib(z, q).start()

    away = side_rows(1 - side)
    leg_load.wait()
    for q in range(chunks):
        cut = slice(q * width, (q + 1) * width)
        leg_away[:, cut] = jnp.dot(away, leg_v[:, cut], preferred_element_type=F32).astype(BF16)
        leg_copy(q).start()

    here = side_rows(side)
    for q in range(chunks):
        cut = slice(q * width, (q + 1) * width)
        leg_here[0, :, cut] = jnp.dot(here, leg_v[:, cut], preferred_element_type=F32).astype(BF16)

    def below(d, q):
        arrive(2 * (z - d) + core, q)

        @pl.when(z < depth - 1)
        def _():
            to_up(z - d, q).start()

        to_sib(z - d, q).start()

    def above(d, q):
        arrive(2 * (z + d) + core, q)

        @pl.when(z > 0)
        def _():
            to_down(z + d, q).start()

        to_sib(z + d, q).start()

    for d in range(1, depth):
        for q in range(chunks):
            pl.when(z >= d)(functools.partial(below, d, q))
            pl.when(z <= depth - 1 - d)(functools.partial(above, d, q))
    for q in range(chunks):
        leg_copy(q).wait_recv()
    for zz in range(depth):
        for q in range(chunks):
            arrive(2 * zz + 1 - core, q)

    row_pos = split_index(iota((rows_half, span), 0), line)[1]
    same = row_pos == split_index(iota((rows_half, span), 1), cols)[0]
    gather_rows = jnp.where(
        iota((cycles, rows_half), 0) == split_index(iota((cycles, rows_half), 1), line)[0], 1.0, 0.0
    ).astype(BF16)

    def apply(which):
        cross = jnp.zeros((rows_half, span), F32)
        for q in range(chunks):
            cross += lax.dot_general(
                leg_here[which, :, q * width : (q + 1) * width],
                gathered[q].reshape(span, width),
                (((1,), (1,)), ((), ())),
                preferred_element_type=F32,
            )
        own = jnp.where(same, cross, 0.0).astype(BF16)
        return jnp.dot(gather_rows, own, preferred_element_type=F32).astype(BF16)

    harm_copy = pltpu.make_async_remote_copy(
        src_ref=harm_away,
        dst_ref=harm.at[side],
        send_sem=harm_sem.at[0],
        recv_sem=harm_sem.at[1],
        device_id={"mset": partner},
        device_id_type=MESH,
    )
    harm_away[...] = apply(1)
    harm_copy.start()
    harm[side] = apply(0)
    for zz in range(depth):
        for q in range(chunks):
            to_sib(zz, q).wait_send()

            @pl.when((z < depth - 1) & (zz <= z))
            def _():
                to_up(zz, q).wait_send()

            @pl.when((z > 0) & (zz >= z))
            def _():
                to_down(zz, q).wait_send()

    for q in range(chunks):
        leg_copy(q).wait_send()

    row_cycle, _ = split_index(iota((rows_out, cycles), 0), REAL)
    repeat = jnp.where(row_cycle == iota((rows_out, cycles), 1), 1.0, 0.0).astype(BF16)
    row_s = split_index(iota((rows_out, span), 0), REAL)[1]
    col_s = split_index(iota((rows_out, span), 1), REAL)[1]
    keep = row_s == col_s
    src_pos, src_c = split_index(iota((span, 2 * subset), 0), cols)
    src_zz, src_core = split_index(src_pos, 2)
    dst_part, dst_m = split_index(iota((span, 2 * subset), 1), subset)
    same_part = split_index(src_c, REAL)[0] == dst_part
    harm_copy.wait()
    total = jnp.zeros((rows_out, 2 * subset), F32)
    for which in range(2):
        spread = jnp.dot(repeat, harm[which], preferred_element_type=F32)
        picked = jnp.where(keep, spread, 0.0).astype(BF16)
        hit = same_part & (src_zz * group + which * 2 + src_core == dst_m)
        select = jnp.where(hit, 1.0, 0.0).astype(BF16)
        total += jnp.dot(picked, select, preferred_element_type=F32)
    out_ref[...] = total.astype(BF16)


def synthesis_kernel(tiles, scale, m_ref, h_ref, out_ref, h_v, table, buf, sem):
    subset = m_ref.shape[0]
    tile = out_ref.shape[1] // tiles
    load = pltpu.make_async_copy(h_ref, h_v, sem.at[tiles])
    load.start()
    m_col = jnp.zeros((subset, LANES), jnp.int32)
    slot = iota((subset, LANES), 0)
    for i in range(subset):
        m_col = jnp.where(slot == i, m_ref[i], m_col)
    lane = iota((subset, LANES), 1)
    fine = split_index(m_col * lane, NPHI)[1].astype(F32) * (2.0 * math.pi / NPHI)
    coarse = split_index(m_col * (lane * LANES), NPHI)[1].astype(F32) * (2.0 * math.pi / NPHI)
    fine_cos, fine_sin = jnp.cos(fine), jnp.sin(fine)
    coarse_cos, coarse_sin = jnp.cos(coarse), jnp.sin(coarse)

    def fill(t):
        for a in range(t * tile // LANES, (t + 1) * tile // LANES):
            c = coarse_cos[:, a : a + 1]
            s = coarse_sin[:, a : a + 1]
            table[0:subset, a * LANES : (a + 1) * LANES] = (c * fine_cos - s * fine_sin).astype(BF16)
            table[subset : 2 * subset, a * LANES : (a + 1) * LANES] = (
                -(s * fine_cos + c * fine_sin)
            ).astype(BF16)

    copies = []
    fill(0)
    load.wait()
    for t in range(tiles):
        cut = slice(t * tile, (t + 1) * tile)
        total = jnp.dot(h_v[...], table[:, cut], preferred_element_type=F32)
        buf[:, cut] = (total * scale).astype(BF16)
        copies.append(pltpu.make_async_copy(buf.at[:, cut], out_ref.at[:, cut], sem.at[t]))
        copies[-1].start()
        if t + 1 < tiles:
            fill(t + 1)
    for c in copies:
        c.wait()


def body(n, m_list, coeff, blocks, legendre):
    per_device, cols, order_max = coeff.shape
    assert per_device == 1 and n % 4 == 0
    cycles, subset, _ = legendre.shape
    chunks = 3
    depth = n // 4
    rows_in, rows_out = cycles * subset, cycles * REAL
    vmem = pl.BlockSpec(memory_space=pltpu.VMEM)
    hbm = pl.BlockSpec(memory_space=pl.ANY)
    dma = pltpu.SemaphoreType.DMA
    harmonics = pl.pallas_call(
        functools.partial(harmonics_kernel, n, chunks),
        out_shape=jax.ShapeDtypeStruct((rows_out, 2 * subset), BF16),
        in_specs=[pl.BlockSpec(memory_space=pltpu.SMEM), hbm, hbm, hbm],
        out_specs=vmem,
        scratch_shapes=[
            pltpu.VMEM((cols, order_max), BF16),
            pltpu.VMEM((chunks, order_max, order_max // chunks), BF16),
            pltpu.VMEM((rows_in, order_max), BF16),
            pltpu.VMEM((rows_in // 2, order_max), BF16),
            pltpu.VMEM((2, rows_in // 2, order_max), BF16),
            pltpu.VMEM((chunks, n // 2, cols, order_max // chunks), BF16),
            pltpu.VMEM((cycles, n // 2 * cols), BF16),
            pltpu.VMEM((2, cycles, n // 2 * cols), BF16),
            dma((chunks + 2,)),
            dma((chunks, n // 2)),
            dma((chunks, depth)),
            dma((chunks, depth)),
            dma((chunks, depth)),
            dma((chunks,)),
            dma((chunks,)),
            dma((2,)),
        ],
        compiler_params=pltpu.CompilerParams(collective_id=0, has_side_effects=True),
        name="harmonics",
    )(m_list, coeff, blocks, legendre.reshape(rows_in, order_max))
    tiles = 8
    sky = pl.pallas_call(
        functools.partial(synthesis_kernel, tiles, 1.0 / math.sqrt(subset)),
        out_shape=jax.ShapeDtypeStruct((rows_out, NPHI), BF16),
        in_specs=[pl.BlockSpec(memory_space=pltpu.SMEM), hbm],
        out_specs=hbm,
        scratch_shapes=[
            pltpu.VMEM((rows_out, 2 * subset), BF16),
            pltpu.VMEM((2 * subset, NPHI), BF16),
            pltpu.VMEM((rows_out, NPHI), BF16),
            dma((tiles + 1,)),
        ],
        name="synthesis",
    )(m_list, harmonics)
    return sky.reshape(cycles, REAL, NPHI)


def solution(mesh):
    spec = P(("groups", "mset"), None, None)
    return jax.shard_map(
        functools.partial(body, mesh.shape["mset"]),
        mesh=mesh,
        in_specs=(P(), spec, spec, spec),
        out_specs=spec,
        check_vma=False,
    )
```

time: 25.9 us -> 25 us (0.965)
  the two profiles are of different devices: /device:TPU:1 before, /device:TPU:0 now
where the time goes in v2:
time: 25 us; the launch traced here: 24.8 us
  Pallas kernels  24.8 us (99%)
    pallas_call x1, Pallas kernels, body(): pl.pallas_call(functools.partial(harmonics_kernel, n, chunks), out_shape=...  20.9 us
    pallas_call x1, Pallas kernels, body(): pl.pallas_call(functools.partial(synthesis_kernel, tiles, 1.0 / math.sqrt...  3.88 us

profile of v2, /device:TPU:0, one launch (start us, length us, event | category | flops | bytes accessed | tf_op | source)
XLA Modules:
  0.0 24.8 jit_solution(16823731141982653422)
XLA Ops:
  0.0 20.9 %harmonics.1.h_ref = bf16[256,32]{1,0:T(8,128)(2,1)} custom-call(s32[16]{0:T(128)} %m_ref.3, bf16[1,32,1536]{2,1,0:T(8,128)(2,1)} %coeff_ref.1, bf16[1,1536,1536]{2,1,0:T(8,128)(2,1)} %blocks_ref.1, bf16[256,1536]{1,0:T(8,128)(2,1)} %bitcast.2), custom_call_target="tpu_custom_call" | custom-call | tf_op jit(solution)/shard_map/harmonics/pallas_call | solution.py:300
  20.9 3.9 %synthesis.1 = bf16[256,8192]{1,0:T(8,128)(2,1)} custom-call(s32[16]{0:T(128)} %m_ref.3, bf16[256,32]{1,0:T(8,128)(2,1)} %harmonics.1.h_ref), custom_call_target="tpu_custom_call" | custom-call | tf_op jit(solution)/shard_map/synthesis/pallas_call | solution.py:327

commit v3 on v2

--- a/solution.py
+++ b/solution.py
@@ -248,11 +248,9 @@
     out_ref[...] = total.astype(BF16)
 
 
-def synthesis_kernel(tiles, scale, m_ref, h_ref, out_ref, h_v, table, buf, sem):
+def synthesis_kernel(tiles, scale, m_ref, h_v, out_ref, table, buf, sem):
     subset = m_ref.shape[0]
     tile = out_ref.shape[1] // tiles
-    load = pltpu.make_async_copy(h_ref, h_v, sem.at[tiles])
-    load.start()
     m_col = jnp.zeros((subset, LANES), jnp.int32)
     slot = iota((subset, LANES), 0)
     for i in range(subset):
@@ -274,7 +272,6 @@
 
     copies = []
     fill(0)
-    load.wait()
     for t in range(tiles):
         cut = slice(t * tile, (t + 1) * tile)
         total = jnp.dot(h_v[...], table[:, cut], preferred_element_type=F32)
@@ -294,8 +291,9 @@
     chunks = 3
     depth = n // 4
     rows_in, rows_out = cycles * subset, cycles * REAL
+    keep = functools.partial(pltpu.with_memory_space_constraint, memory_space=pltpu.HBM)
     vmem = pl.BlockSpec(memory_space=pltpu.VMEM)
-    hbm = pl.BlockSpec(memory_space=pl.ANY)
+    hbm = pl.BlockSpec(memory_space=pltpu.HBM)
     dma = pltpu.SemaphoreType.DMA
     harmonics = pl.pallas_call(
         functools.partial(harmonics_kernel, n, chunks),
@@ -320,22 +318,21 @@
             dma((chunks,)),
             dma((2,)),
         ],
-        compiler_params=pltpu.CompilerParams(collective_id=0, has_side_effects=True),
+        compiler_params=pltpu.CompilerParams(collective_id=0, has_side_effects=True, vmem_limit_bytes=40 << 20),
         name="harmonics",
-    )(m_list, coeff, blocks, legendre.reshape(rows_in, order_max))
+    )(m_list, keep(coeff), keep(blocks), keep(legendre.reshape(rows_in, order_max)))
     tiles = 8
     sky = pl.pallas_call(
         functools.partial(synthesis_kernel, tiles, 1.0 / math.sqrt(subset)),
         out_shape=jax.ShapeDtypeStruct((rows_out, NPHI), BF16),
-        in_specs=[pl.BlockSpec(memory_space=pltpu.SMEM), hbm],
+        in_specs=[pl.BlockSpec(memory_space=pltpu.SMEM), vmem],
         out_specs=hbm,
         scratch_shapes=[
-            pltpu.VMEM((rows_out, 2 * subset), BF16),
             pltpu.VMEM((2 * subset, NPHI), BF16),
             pltpu.VMEM((rows_out, NPHI), BF16),
-            dma((tiles + 1,)),
+            dma((tiles,)),
         ],
-        name="synthesis",
+        name="synthesis", compiler_params=pltpu.CompilerParams(vmem_limit_bytes=40 << 20),
     )(m_list, harmonics)
     return sky.reshape(cycles, REAL, NPHI)
 

time: 25 us -> 24 us (0.960)
  Pallas kernels: 24.8 us -> 23.2 us
  local copies, waits for them, and re-layouts: 0 us -> 0.65 us
    pallas_call x1, Pallas kernels: 3.88 us -> 3.06 us  [body(): pl.pallas_call(functools.partial(synthesis_kernel, tiles, 1.0 / math.sqrt...]
    pallas_call x1, Pallas kernels: 20.9 us -> 20.2 us  [body(): pl.pallas_call(functools.partial(harmonics_kernel, n, chunks), out_shape=...]
    unnamed x0 -> x2, local copies, waits for them, and re-layouts: none -> 0.65 us
where the time goes in v3:
time: 24 us; the launch traced here: 23.9 us
  Pallas kernels  23.2 us (97%)
  local copies, waits for them, and re-layouts  0.65 us (3%)
    pallas_call x1, Pallas kernels, body(): pl.pallas_call(functools.partial(harmonics_kernel, n, chunks), out_shape=...  20.2 us
    pallas_call x1, Pallas kernels, body(): pl.pallas_call(functools.partial(synthesis_kernel, tiles, 1.0 / math.sqrt...  3.06 us
    unnamed x2, local copies, waits for them, and re-layouts  0.65 us

profile of v3, /device:TPU:0, one launch (start us, length us, event | category | flops | bytes accessed | tf_op | source)
XLA Modules:
  0.0 23.9 jit_solution(12562117789910486519)
XLA Ops:
  0.0 0.0 copy-start
  0.0 0.7 %copy-done = s32[16]{0:T(128)S(1)} copy-done((s32[16]{0:T(128)S(1)}, s32[16]{0:T(128)}, u32[]{:S(2)}) %copy-start) | copy-done | bytes 88
  0.7 20.2 %harmonics.1.h_v = bf16[256,32]{1,0:T(8,128)(2,1)S(1)} custom-call(s32[16]{0:T(128)S(1)} %copy-done, bf16[1,32,1536]{2,1,0:T(8,128)(2,1)} %coeff_ref.1, bf16[1,1536,1536]{2,1,0:T(8,128)(2,1)} %blocks_ref.1, bf16[256,1536]{1,0:T(8,128)(2,1)} %bitcast.2), custom_call_target="tpu_custom_call" | custom-call | tf_op jit(solution)/shard_map/harmonics/pallas_call | solution.py:298
  20.8 3.1 %synthesis.1 = bf16[256,8192]{1,0:T(8,128)(2,1)} custom-call(s32[16]{0:T(128)S(1)} %copy-done, bf16[256,32]{1,0:T(8,128)(2,1)S(1)} %harmonics.1.h_v), custom_call_target="tpu_custom_call" | custom-call | tf_op jit(solution)/shard_map/synthesis/pallas_call | solution.py:325
Async XLA Ops:
  0.0 0.7 %copy-start = (s32[16]{0:T(128)S(1)}, s32[16]{0:T(128)}, u32[]{:S(2)}) copy-start(s32[16]{0:T(128)} %m_ref.3) | copy-start | bytes 196
